TPU v7x, 256 devices: a whole 4x4x8 slice. The times are simulated.
256 devices in a mesh: expert: 64 (over y, z, core), dp: 4 (over x).
Axes of the slice: x: 4, y: 4, z: 8, core: 2. Of those that a mesh axis runs over, the one named last changes fastest.
Arguments:
- tokens: bfloat16 [32768, 1440], P(('expert', 'dp')), may hold values from -6 to 6
- routes: int32 [32768, 4], P(('expert', 'dp')), may hold values from 0 to 63, as said below
- gate_fixed: int32 [32768, 4], P(('expert', 'dp')), may hold values from 4096 to 65535
- counts: int32 [256], P(('expert', 'dp')), may hold values from 32 to 128, as said below
- replica_plan: int32 [8], replicated, may hold values from 0 to 63, as said below
- weight_in: bfloat16 [64, 1440, 1440], P('expert', None, 'dp'), may hold values from -0.15625 to 0.15625
- weight_out: bfloat16 [64, 1440, 1440], P('expert', 'dp'), may hold values from -0.15625 to 0.15625
- cotangent: bfloat16 [32768, 1440], P(('expert', 'dp')), may hold values from -0.59765625 to 0.59765625
Outputs:
- layer_output: bfloat16 [32768, 1440], P(('expert', 'dp'))
- input_grads: bfloat16 [32768, 1440], P(('expert', 'dp'))
- weight_in_grad: bfloat16 [64, 1440, 1440], P('expert', None, 'dp')
- weight_out_grad: bfloat16 [64, 1440, 1440], P('expert', 'dp')
Inputs may be any that keep to these rules, and one draw needn't show every extreme that they name: `routes`: each row names 4 different experts. `replica_plan`: 8 different experts, among them 0, 31, 32 and 63, in any order. `counts`: some device has 128 live tokens in every draw.
All inputs are finite; a program needn't handle non-finite values.
Results may differ from a plain program's by a relative error of at most 0.0064.
Values may be sent and summed in bfloat16 or wider, within the bound.
No kernel may reach another device: no remote copies, remote signals or barrier semaphores. Data moves between devices by JAX's collectives and lax.ppermute only.
A program may use at most 128 MiB of HBM per device.

v0:
```python
import jax
import jax.numpy as jnp
from jax import lax
from jax.sharding import PartitionSpec as P


def shifted(value, axis, steps):
    count = lax.axis_size(axis)
    pairs = [(source, (source + steps) % count) for source in range(count)]
    return lax.ppermute(value, axis, pairs)


def activate(values):
    return values * jax.nn.sigmoid(1.702 * values)


def derivative(values):
    sigmoid_value = jax.nn.sigmoid(1.702 * values)
    return sigmoid_value + 1.702 * values * sigmoid_value * (1.0 - sigmoid_value)


def slot_tables(routes, live_count, frequent_indicator, experts, capacity, spare_slots):
    token_count, top_count = routes.shape
    slot_width = capacity + spare_slots
    active = (jnp.arange(token_count, dtype=jnp.int32) < live_count).astype(jnp.int32)
    flattened = routes.reshape(-1)
    active_flat = jnp.repeat(active, top_count, total_repeat_length=token_count * top_count)
    same_expert = (flattened[:, None] == jnp.arange(experts, dtype=jnp.int32)[None, :]).astype(
        jnp.int32
    )
    matches = same_expert * active_flat[:, None]
    before = jnp.cumsum(matches, axis=0) - matches
    position = jnp.sum(before * matches, axis=1)
    hot_route = jnp.sum(same_expert * frequent_indicator[None, :], axis=1)
    keep_route = (active_flat > 0) & (position < capacity + spare_slots * hot_route)
    target_block = jnp.where(position < capacity, flattened, (flattened + experts // 2) % experts)
    slot_index = jnp.where(keep_route, target_block * slot_width + position, experts * slot_width)
    source = jnp.full((experts * slot_width + 1,), -1, jnp.int32)
    source = source.at[slot_index].set(jnp.arange(token_count * top_count, dtype=jnp.int32))
    return (slot_index, source[: experts * slot_width])


def gather_back(returned, slot_index, features):
    flattened = returned.reshape(-1, features)
    padded = jnp.concatenate([flattened, jnp.zeros((1, features), flattened.dtype)], axis=0)
    return padded[slot_index].astype(jnp.float32)


def slot_products(stacked, own_weight, copy_weight, dims, capacity, amount):
    width = stacked.shape[2]
    own_part = stacked[:, :capacity].reshape(-1, width)
    copy_part = stacked[:, capacity:].reshape(-1, width)
    own_term = lax.dot_general(own_part, own_weight, dims, preferred_element_type=jnp.float32)
    copy_term = lax.dot_general(copy_part, copy_weight, dims, preferred_element_type=jnp.float32)
    return jnp.concatenate(
        [
            own_term.reshape(amount, capacity, -1),
            copy_term.reshape(amount, stacked.shape[1] - capacity, -1),
        ],
        axis=1,
    )


def on_device(tokens, routes, gate_fixed, counts, replica_plan, weight_in, weight_out, cotangent):
    token_count, features = tokens.shape
    top_count = routes.shape[1]
    groups = lax.axis_size("expert")
    experts = groups * weight_in.shape[0]
    capacity = 3 * token_count * top_count // (8 * experts)
    spare_slots = capacity // 2
    slot_width = capacity + spare_slots
    contract_first = (((0,), (0,)), ((), ()))
    contract_last = (((1,), (1,)), ((), ()))
    contract_plain = (((1,), (0,)), ((), ()))
    frequent_indicator = jnp.sum(
        (replica_plan[:, None] == jnp.arange(experts, dtype=jnp.int32)[None, :]).astype(jnp.int32),
        axis=0,
    )
    slot_index, source = slot_tables(
        routes, counts[0], frequent_indicator, experts, capacity, spare_slots
    )
    filled = (source >= 0)[:, None]
    route_ids = jnp.maximum(source, 0)
    token_ids = route_ids // top_count
    scales = gate_fixed.reshape(-1).astype(jnp.float32) / 65536.0
    sent_rows = jnp.where(filled, tokens[token_ids], jnp.zeros((), jnp.bfloat16)).reshape(
        experts, slot_width, features
    )
    grad_rows = jnp.where(
        filled, scales[route_ids][:, None] * cotangent[token_ids].astype(jnp.float32), 0.0
    )
    grad_rows = grad_rows.astype(jnp.bfloat16).reshape(experts, slot_width, features)
    slab_in, slab_out = shifted((weight_in, weight_out), "expert", groups // 2)
    w_first = weight_in[0]
    w_second = weight_out[0]
    copy_first = slab_in[0]
    copy_second = slab_out[0]
    inbound = lax.all_to_all(sent_rows, "expert", split_axis=0, concat_axis=0, tiled=True)
    all_in = lax.all_gather(inbound, "dp", axis=0, tiled=True)
    blocks = all_in.shape[0]
    own_rows = all_in[:, :capacity].reshape(-1, features)
    copy_rows = all_in[:, capacity:].reshape(-1, features)
    own_pre = jnp.dot(own_rows, w_first, preferred_element_type=jnp.float32)
    copy_pre = jnp.dot(copy_rows, copy_first, preferred_element_type=jnp.float32)
    own_act = activate(own_pre).astype(jnp.bfloat16)
    copy_act = activate(copy_pre).astype(jnp.bfloat16)
    hidden_share = own_act.shape[1]
    act_all = jnp.concatenate(
        [
            own_act.reshape(blocks, capacity, hidden_share),
            copy_act.reshape(blocks, spare_slots, hidden_share),
        ],
        axis=1,
    )
    outputs = lax.psum_scatter(
        slot_products(
            act_all, w_second, copy_second, contract_plain, capacity, groups * lax.axis_size("dp")
        ),
        "dp",
        scatter_dimension=0,
        tiled=True,
    ).astype(jnp.bfloat16)
    returned = lax.all_to_all(outputs, "expert", split_axis=0, concat_axis=0, tiled=True)
    inbound_grad = lax.all_to_all(grad_rows, "expert", split_axis=0, concat_axis=0, tiled=True)
    all_grad = lax.all_gather(inbound_grad, "dp", axis=0, tiled=True)
    own_grad = all_grad[:, :capacity].reshape(-1, features)
    copy_grad = all_grad[:, capacity:].reshape(-1, features)
    own_act_grad = lax.dot_general(
        own_grad, w_second, contract_last, preferred_element_type=jnp.float32
    )
    copy_act_grad = lax.dot_general(
        copy_grad, copy_second, contract_last, preferred_element_type=jnp.float32
    )
    own_pre_grad = (own_act_grad * derivative(own_pre)).astype(jnp.bfloat16)
    copy_pre_grad = (copy_act_grad * derivative(copy_pre)).astype(jnp.bfloat16)
    pre_all = jnp.concatenate(
        [
            own_pre_grad.reshape(blocks, capacity, hidden_share),
            copy_pre_grad.reshape(blocks, spare_slots, hidden_share),
        ],
        axis=1,
    )
    input_rows = lax.psum_scatter(
        slot_products(
            pre_all, w_first, copy_first, contract_last, capacity, groups * lax.axis_size("dp")
        ),
        "dp",
        scatter_dimension=0,
        tiled=True,
    ).astype(jnp.bfloat16)
    copy_term_second = lax.dot_general(
        copy_act, copy_grad, contract_first, preferred_element_type=jnp.float32
    )
    copy_term_first = lax.dot_general(
        copy_rows, copy_pre_grad, contract_first, preferred_element_type=jnp.float32
    )
    home_second, home_first = (
        shifted(copy_term_second.astype(jnp.bfloat16), "expert", groups // 2).astype(
            copy_term_second.dtype
        ),
        shifted(copy_term_first.astype(jnp.bfloat16), "expert", groups // 2).astype(
            copy_term_first.dtype
        ),
    )
    grad_second = (
        lax.dot_general(own_act, own_grad, contract_first, preferred_element_type=jnp.float32)
        + home_second
    )
    grad_first = (
        lax.dot_general(own_rows, own_pre_grad, contract_first, preferred_element_type=jnp.float32)
        + home_first
    )
    weight_out_grad = grad_second.astype(jnp.bfloat16)[None]
    weight_in_grad = grad_first.astype(jnp.bfloat16)[None]
    returned_grad = lax.all_to_all(input_rows, "expert", split_axis=0, concat_axis=0, tiled=True)
    picked = gather_back(returned, slot_index, features) * scales[:, None]
    layer_output = jnp.sum(picked.reshape(token_count, top_count, features), axis=1).astype(
        jnp.bfloat16
    )
    picked_grad = gather_back(returned_grad, slot_index, features)
    input_grads = jnp.sum(picked_grad.reshape(token_count, top_count, features), axis=1).astype(
        jnp.bfloat16
    )
    return (layer_output, input_grads, weight_in_grad, weight_out_grad)


def solution(mesh):
    return jax.shard_map(
        on_device,
        mesh=mesh,
        in_specs=(
            P(("expert", "dp"), None),
            P(("expert", "dp"), None),
            P(("expert", "dp"), None),
            P(("expert", "dp")),
            P(),
            P("expert", None, "dp"),
            P("expert", "dp", None),
            P(("expert", "dp"), None),
        ),
        out_specs=(
            P(("expert", "dp"), None),
            P(("expert", "dp"), None),
            P("expert", None, "dp"),
            P("expert", "dp", None),
        ),
        check_vma=False,
    )
```

profile of v0, /device:TPU:1, one launch (start us, length us, event | category | flops | bytes accessed | tf_op | source)
XLA Modules:
  0.0 530.6 jit_solution(11869775184831770626)
XLA Ops:
  8.7 3.3 gather_fusion
  21.8 36.2 %all_to_all.20 = bf16[64,4,1440]{2,1,0:T(4,128)(2,1)} all-to-all(bf16[64,4,1440]{2,1,0:T(4,128)(2,1)S(1)} %select_convert_fusion), channel_id=1, replica_groups=mesh['expert'=64,'dp'=4] {'expert'}, dimensions={0} | all-to-all | bytes 1474560 | tf_op jit(solution)/shard_map/all_to_all | solution.py:124
  60.1 29.1 %all_to_all.21 = bf16[64,4,1440]{2,1,0:T(4,128)(2,1)} all-to-all(bf16[64,4,1440]{2,1,0:T(4,128)(2,1)S(1)} %broadcast_select_fusion), channel_id=1, replica_groups=mesh['expert'=64,'dp'=4] {'expert'}, dimensions={0} | all-to-all | bytes 1474560 | tf_op jit(solution)/shard_map/all_to_all | solution.py:98
  93.5 3.5 all-gather.5.cloned.1.call-done
  97.1 3.6 slice.60
  100.7 3.3 copy.76
  104.0 37.2 %all-gather.3.cloned.1.call-done = bf16[256,4,1440]{2,1,0:T(4,128)(2,1)} async-done(((bf16[64,4,1440]{2,1,0:T(4,128)(2,1)}), bf16[256,4,1440]{2,1,0:T(4,128)(2,1)}) %all-gather.3.cloned.1.call-update) | async-done | bytes 2949136 | tf_op jit(solution)/shard_map/all_gather | solution.py:99
  141.2 4.9 slice.58
  146.1 4.6 copy.75
  150.7 4.1 reshape.318
  154.8 5.4 %reshape.314 = bf16[768,1440]{1,0:T(8,128)(2,1)S(1)} reshape(bf16[256,3,1440]{2,1,0:T(4,128)(2,1)} %bitcast.86) | data formatting | bytes 4423680 | tf_op jit(solution)/shard_map/reshape | solution.py:101
  160.2 3.3 multiply_convert_fusion
  179.4 7.9 %copy.70 = f32[256,4,1440]{2,1,0:T(4,128)} copy(f32[256,4,1440]{0,2,1:T(8,128)} %pad_maximum_fusion.1) | data formatting | bytes 11796480 | tf_op jit(solution)/shard_map/concatenate | solution.py:55
  194.7 7.8 %copy.63 = f32[256,4,1440]{2,1,0:T(4,128)} copy(f32[256,4,1440]{0,2,1:T(8,128)} %pad_maximum_fusion) | data formatting | bytes 11796480 | tf_op jit(solution)/shard_map/concatenate | solution.py:55
  202.5 215.7 %all-reduce.6 = (bf16[256,4,1440]{2,1,0:T(4,128)(2,1)}, bf16[256,4,1440]{2,1,0:T(4,128)(2,1)}) all-reduce(f32[256,4,1440]{2,1,0:T(4,128)} %copy.63, f32[256,4,1440]{2,1,0:T(4,128)} %copy.70), channel_id=2, replica_groups=mesh['expert'=64,'dp'=4] {'dp'}, use_global_device_ids=true, to_apply=%region_6.7.clone | all-reduce | flops 2949120 | bytes 17694720
  420.4 12.4 %all-to-all-start.1 = ((bf16[64,4,1440]{2,1,0:T(4,128)(2,1)}), bf16[64,4,1440]{2,1,0:T(4,128)(2,1)S(1)}, u32[]{:S(2)}, u32[]{:S(2)}) async-start(bf16[64,4,1440]{2,1,0:T(4,128)(2,1)} %dynamic-slice_convert_fusion.1), calls=%async_computation.1 | async-start | bytes 1572864 | tf_op jit(solution)/shard_map/all_to_all | solution.py:123
  439.6 16.1 %all-to-all-done.1 = bf16[64,4,1440]{2,1,0:T(4,128)(2,1)S(1)} async-done(((bf16[64,4,1440]{2,1,0:T(4,128)(2,1)}), bf16[64,4,1440]{2,1,0:T(4,128)(2,1)S(1)}, u32[]{:S(2)}, u32[]{:S(2)}) %all-to-all-start.1) | async-done | bytes 737312 | tf_op jit(solution)/shard_map/all_to_all | solution.py:123
  455.8 6.2 %all-to-all-start.3 = ((bf16[64,4,1440]{2,1,0:T(4,128)(2,1)}), bf16[64,4,1440]{2,1,0:T(4,128)(2,1)S(1)}, u32[]{:S(2)}, u32[]{:S(2)}) async-start(bf16[64,4,1440]{2,1,0:T(4,128)(2,1)} %dynamic-slice_convert_fusion), calls=%async_computation.3 | async-start | bytes 1572864 | tf_op jit(solution)/shard_map/all_to_all | solution.py:175
  462.6 3.1 collective-permute-start.2
  465.7 4.0 collective-permute-done.3
  469.7 4.0 fusion.3
  473.7 27.4 %collective-permute-done.2 = bf16[1440,360]{1,0:T(8,128)(2,1)S(1)} collective-permute-done((bf16[1440,360]{1,0:T(8,128)(2,1)S(1)}, bf16[1440,360]{1,0:T(8,128)(2,1)S(1)}, u32[]{:S(2)}, u32[]{:S(2)}) %collective-permute-start.2) | collective-permute-done | bytes 1036832 | tf_op jit(solution)/shard_map/ppermute | solution.py:10
  504.4 3.2 gather_fusion.5
  519.5 3.1 multiply_reduce_fusion
  (119 shorter events, 65.0 us)
Async XLA Ops:
  7.2 4.9 copy-start.15
  7.2 5.0 copy-start.16
  7.2 5.5 %copy-start.18 = (s32[8]{0:T(128)S(1)}, s32[8]{0:T(128)}, u32[]{:S(2)}) copy-start(s32[8]{0:T(128)} %param.14) | copy-start | bytes 100
  7.2 89.9 %all-gather.5.cloned.1.call-start = ((), (), s32[]{:S(2)}) async-start(), calls=%async_computation.5 | async-start | bytes 3932160 | tf_op jit(solution)/shard_map/all_gather | solution.py:125
  8.7 8.2 %copy-start.17 = (s32[128,4]{0,1:T(4,128)S(1)}, s32[128,4]{0,1:T(4,128)}, u32[]{:S(2)}) copy-start(s32[128,4]{0,1:T(4,128)} %param.12) | copy-start | bytes 6148
  12.1 7.3 %copy-start.13 = (bf16[128,1440]{0,1:T(8,128)(2,1)S(1)}, bf16[128,1440]{0,1:T(8,128)(2,1)}, u32[]{:S(2)}) copy-start(bf16[128,1440]{0,1:T(8,128)(2,1)} %param.17) | copy-start | bytes 1105924
  21.8 36.3 %copy-start.14 = (bf16[128,1440]{0,1:T(8,128)(2,1)S(1)}, bf16[128,1440]{0,1:T(8,128)(2,1)}, u32[]{:S(2)}) copy-start(bf16[128,1440]{0,1:T(8,128)(2,1)} %param.10) | copy-start | bytes 1105924
  58.0 83.2 %all-gather.3.cloned.1.call-start = ((), (), s32[]{:S(2)}) async-start(), calls=%async_computation.4 | async-start | bytes 3932160 | tf_op jit(solution)/shard_map/all_gather | solution.py:99
  60.1 32.2 %copy-start.19 = (u32[256]{0:T(256)S(1)}, u32[256]{0:T(256)}, u32[]{:S(2)}) copy-start(u32[256]{0:T(256)} %constant.170) | copy-start | bytes 3076
  89.2 78.8 %collective-permute-start = (bf16[1,1440,360]{2,1,0:T(8,128)(2,1)}, bf16[1,1440,360]{2,1,0:T(8,128)(2,1)}, u32[]{:S(2)}, u32[]{:S(2)}) collective-permute-start(bf16[1,1440,360]{2,1,0:T(8,128)(2,1)} %param.15), channel_id=1, source_target_pairs={{0,128},{4,132},{8,136},{12,140},{16,144},{20,148},{24,152},{28,15... | collective-permute-start | bytes 3110408 | tf_op jit(solution)/shard_map/ppermute | solution.py:10
  92.1 80.8 %collective-permute-start.1 = (bf16[1,360,1440]{2,1,0:T(8,128)(2,1)}, bf16[1,360,1440]{2,1,0:T(8,128)(2,1)}, u32[]{:S(2)}, u32[]{:S(2)}) collective-permute-start(bf16[1,360,1440]{2,1,0:T(8,128)(2,1)} %param.16), channel_id=1, source_target_pairs={{0,128},{4,132},{8,136},{12,140},{16,144},{20,148},{24,152},{28,15... | collective-permute-start | bytes 3110408 | tf_op jit(solution)/shard_map/ppermute | solution.py:10
  141.2 9.5 %copy-start = (bf16[256,4,1440]{2,1,0:T(4,128)(2,1)S(1)}, bf16[256,4,1440]{2,1,0:T(4,128)(2,1)}, u32[]{:S(2)}) copy-start(bf16[256,4,1440]{2,1,0:T(4,128)(2,1)} %all-gather.5.cloned.1.call-done) | copy-start | bytes 8847364
  160.2 3.3 copy-start.2
  160.2 3.4 copy-start.4
  163.5 3.0 copy-start.11
  174.6 4.8 copy-start.6
  420.4 35.3 %all-to-all-start.1 = ((bf16[64,4,1440]{2,1,0:T(4,128)(2,1)}), bf16[64,4,1440]{2,1,0:T(4,128)(2,1)S(1)}, u32[]{:S(2)}, u32[]{:S(2)}) async-start(bf16[64,4,1440]{2,1,0:T(4,128)(2,1)} %dynamic-slice_convert_fusion.1), calls=%async_computation.1 | async-start | bytes 1572864 | tf_op jit(solution)/shard_map/all_to_all | solution.py:123
  434.3 35.4 %collective-permute-start.3 = (bf16[360,1440]{1,0:T(8,128)(2,1)}, bf16[360,1440]{1,0:T(8,128)(2,1)}, u32[]{:S(2)}, u32[]{:S(2)}) collective-permute-start(bf16[360,1440]{1,0:T(8,128)(2,1)} %convolution_convert_fusion.1), channel_id=1, source_target_pairs={{0,128},{4,132},{8,136},{12,140},{16,144},{20,148},{24,152},{28,15... | collective-permute-start | bytes 3110408 | tf_op jit(solution)/shard_map/ppermute | solution.py:10
  437.3 24.7 %copy-start.7 = (bf16[256,360]{0,1:T(8,128)(2,1)S(1)}, bf16[256,360]{0,1:T(8,128)(2,1)}, u32[]{:S(2)}) copy-start(bf16[256,360]{0,1:T(8,128)(2,1)} %copy-done.6) | copy-start | bytes 552964
  439.6 30.0 %copy-start.12 = (bf16[768,360]{0,1:T(8,128)(2,1)S(1)}, bf16[768,360]{0,1:T(8,128)(2,1)}, u32[]{:S(2)}) copy-start(bf16[768,360]{0,1:T(8,128)(2,1)} %copy-done.11) | copy-start | bytes 1658884
  455.8 48.2 %all-to-all-start.3 = ((bf16[64,4,1440]{2,1,0:T(4,128)(2,1)}), bf16[64,4,1440]{2,1,0:T(4,128)(2,1)S(1)}, u32[]{:S(2)}, u32[]{:S(2)}) async-start(bf16[64,4,1440]{2,1,0:T(4,128)(2,1)} %dynamic-slice_convert_fusion), calls=%async_computation.3 | async-start | bytes 1572864 | tf_op jit(solution)/shard_map/all_to_all | solution.py:175
  462.6 38.5 %collective-permute-start.2 = (bf16[1440,360]{1,0:T(8,128)(2,1)S(1)}, bf16[1440,360]{1,0:T(8,128)(2,1)S(1)}, u32[]{:S(2)}, u32[]{:S(2)}) collective-permute-start(bf16[1440,360]{1,0:T(8,128)(2,1)S(1)} %convolution_convert_fusion), channel_id=1, source_target_pairs={{0,128},{4,132},{8,136},{12,140},{16,144},{20,148},{24,152},{28,15... | collective-permute-start | bytes 3110408 | tf_op jit(solution)/shard_map/ppermute | solution.py:10
  465.7 35.4 %copy-start.3 = (bf16[768,1440]{1,0:T(8,128)(2,1)S(1)}, bf16[768,1440]{1,0:T(8,128)(2,1)}, u32[]{:S(2)}) copy-start(bf16[768,1440]{1,0:T(8,128)(2,1)} %copy-done.2) | copy-start | bytes 6635524
  465.7 35.4 %copy-start.10 = (bf16[768,360]{0,1:T(8,128)(2,1)S(1)}, bf16[768,360]{0,1:T(8,128)(2,1)}, u32[]{:S(2)}) copy-start(bf16[768,360]{0,1:T(8,128)(2,1)} %copy-done.9) | copy-start | bytes 1658884
  (4 other events, 6.8 us)
Sparse Core Ops, SparseCore 0:
  58.1 38.9 all-gather.4
  98.9 42.2 all-gather.2
where the time goes:
time: 540 us; the launch traced here: 531 us
  blocking collectives  281 us (52%)
  waiting for transfers between devices  88.3 us (16%)
  local copies, waits for them, and re-layouts  76.1 us (14%)
  starting transfers between devices  27.8 us (5%)
  matrix products  27 us (5%)
  between operations  16.2 us (3%)
  other arithmetic  14.4 us (3%)
    unnamed x1, blocking collectives  216 us
    all_gather x1, waiting for transfers between devices, on_device(): all_in = lax.all_gather(inbound, 'dp', axis=0, tiled=True)  37.2 us
    all_to_all x1, blocking collectives, on_device(): lax.all_to_all(grad_rows, 'expert', split_axis=0, concat_axis=0, tiled=True)  36.2 us
    ppermute x4, waiting for transfers between devices, shifted(): return lax.ppermute(value, axis, pairs)  31.4 us
    all_to_all x1, blocking collectives, on_device(): lax.all_to_all(sent_rows, 'expert', split_axis=0, concat_axis=0, tiled=True)  29.1 us
    all_to_all x1, waiting for transfers between devices, on_device(): lax.all_to_all(outputs, 'expert', split_axis=0, concat_axis=0, tiled=True)  16.1 us
    concatenate x2, local copies, waits for them, and re-layouts, slot_products(): jnp.concatenate([own_term.reshape(amount, capacity, -1), copy_term.reshap...  15.7 us
    all_to_all x1, starting transfers between devices, on_device(): lax.all_to_all(outputs, 'expert', split_axis=0, concat_axis=0, tiled=True)  12.4 us
  transfers between devices with their start and end apart: 8, of which 5 were waited for; matrix products, arithmetic and copies ran while one was open for 10% of the time, Pallas kernels for 0%

commit v1 on v0

--- a/solution.py
+++ b/solution.py
@@ -96,7 +96,14 @@
     copy_first = slab_in[0]
     copy_second = slab_out[0]
     inbound = lax.all_to_all(sent_rows, "expert", split_axis=0, concat_axis=0, tiled=True)
-    all_in = lax.all_gather(inbound, "dp", axis=0, tiled=True)
+    size = lax.axis_size("dp")
+    route = [(i, (i + 1) % size) for i in range(size)]
+    shards = [inbound]
+    for stride in range(1, size):
+        shards = [lax.ppermute(shards[0], "dp", route), *shards]
+    out = jnp.concatenate(shards, axis=0)
+    offset = (lax.axis_index("dp") + 1) * shards[-1].shape[0]
+    all_in = jnp.roll(out, offset, axis=0)
     blocks = all_in.shape[0]
     own_rows = all_in[:, :capacity].reshape(-1, features)
     copy_rows = all_in[:, capacity:].reshape(-1, features)

time: 540 us -> 527 us (0.976)
  blocking collectives: 281 us -> 214 us
  waiting for transfers between devices: 88.3 us -> 115 us
  starting transfers between devices: 27.8 us -> 47.3 us
  local copies, waits for them, and re-layouts: 76.1 us -> 82.4 us
    all_to_all x2 -> x0, blocking collectives: 65.3 us -> none  [the longest x1 36.2 us: on_device(): lax.all_to_all(grad_rows, 'expert', split_axis=0, concat_axis=0, tiled=True)]
    ppermute x0 -> x3, waiting for transfers between devices: none -> 39.8 us  [on_device(): shards = [lax.ppermute(shards[0], 'dp', route), *shards]]
    all_gather x1 -> x0, waiting for transfers between devices: 37.2 us -> none  [on_device(): all_in = lax.all_gather(inbound, 'dp', axis=0, tiled=True)]
    all_to_all x0 -> x2, waiting for transfers between devices: none -> 21 us  [the longest x1 21 us: on_device(): lax.all_to_all(sent_rows, 'expert', split_axis=0, concat_axis=0, tiled=True)]
    all_to_all x0 -> x2, starting transfers between devices: none -> 19.8 us  [the longest x1 13.2 us: on_device(): lax.all_to_all(sent_rows, 'expert', split_axis=0, concat_axis=0, tiled=True)]
    all_to_all x1, waiting for transfers between devices: 16.1 us -> 0.01 us  [on_device(): lax.all_to_all(outputs, 'expert', split_axis=0, concat_axis=0, tiled=True)]
    all_to_all x1, waiting for transfers between devices: 0.01 us -> 16.1 us  [on_device(): lax.all_to_all(input_rows, 'expert', split_axis=0, concat_axis=0, tiled=T...]
    ppermute x4, waiting for transfers between devices: 31.4 us -> 38.5 us  [shifted(): return lax.ppermute(value, axis, pairs)]
  transfers between devices with their start and end apart: 8 -> 12, of which waited for: 5 -> 8; matrix products, arithmetic and copies ran while one was open for 10% -> 12% of each run, Pallas kernels for 0% -> 0%
where the time goes in v1:
time: 527 us; the launch traced here: 517 us
  blocking collectives  214 us (41%)
  waiting for transfers between devices  115 us (22%)
  local copies, waits for them, and re-layouts  82.4 us (16%)
  starting transfers between devices  47.3 us (9%)
  matrix products  25.9 us (5%)
  between operations  16.3 us (3%)
  other arithmetic  16.1 us (3%)
    unnamed x1, blocking collectives  214 us
    ppermute x3, waiting for transfers between devices, on_device(): shards = [lax.ppermute(shards[0], 'dp', route), *shards]  39.8 us
    ppermute x4, waiting for transfers between devices, shifted(): return lax.ppermute(value, axis, pairs)  38.5 us
    all_to_all x1, waiting for transfers between devices, on_device(): lax.all_to_all(sent_rows, 'expert', split_axis=0, concat_axis=0, tiled=True)  21 us
    unnamed x54, local copies, waits for them, and re-layouts  16.8 us
    all_to_all x1, waiting for transfers between devices, on_device(): lax.all_to_all(input_rows, 'expert', split_axis=0, concat_axis=0, tiled=T...  16.1 us
    concatenate x2, local copies, waits for them, and re-layouts, slot_products(): jnp.concatenate([own_term.reshape(amount, capacity, -1), copy_term.reshap...  15.8 us
    all_to_all x1, starting transfers between devices, on_device(): lax.all_to_all(sent_rows, 'expert', split_axis=0, concat_axis=0, tiled=True)  13.2 us
  transfers between devices with their start and end apart: 12, of which 8 were waited for; matrix products, arithmetic and copies ran while one was open for 12% of the time, Pallas kernels for 0%

profile of v1, /device:TPU:1, one launch (start us, length us, event | category | flops | bytes accessed | tf_op | source)
XLA Modules:
  0.0 517.4 jit_solution(2913279683939426923)
XLA Ops:
  8.7 3.3 gather_fusion
  20.0 13.2 %all-to-all-start = ((bf16[64,4,1440]{2,1,0:T(4,128)(2,1)}), bf16[64,4,1440]{2,1,0:T(4,128)(2,1)S(1)}, u32[]{:S(2)}, u32[]{:S(2)}) async-start(bf16[64,4,1440]{2,1,0:T(4,128)(2,1)} %broadcast_select_fusion), calls=%async_computation | async-start | bytes 1572864 | tf_op jit(solution)/shard_map/all_to_all | solution.py:98
  35.2 21.0 %all-to-all-done = bf16[64,4,1440]{2,1,0:T(4,128)(2,1)S(1)} async-done(((bf16[64,4,1440]{2,1,0:T(4,128)(2,1)}), bf16[64,4,1440]{2,1,0:T(4,128)(2,1)S(1)}, u32[]{:S(2)}, u32[]{:S(2)}) %all-to-all-start) | async-done | bytes 737312 | tf_op jit(solution)/shard_map/all_to_all | solution.py:98
  61.0 6.6 %all-to-all-start.2 = ((bf16[64,4,1440]{2,1,0:T(4,128)(2,1)}), bf16[64,4,1440]{2,1,0:T(4,128)(2,1)S(1)}, u32[]{:S(2)}, u32[]{:S(2)}) async-start(bf16[64,4,1440]{2,1,0:T(4,128)(2,1)} %select_convert_fusion), calls=%async_computation.2 | async-start | bytes 1572864 | tf_op jit(solution)/shard_map/all_to_all | solution.py:131
  67.7 8.4 %collective-permute-done = bf16[64,4,1440]{2,1,0:T(4,128)(2,1)S(1)} collective-permute-done((bf16[64,4,1440]{2,1,0:T(4,128)(2,1)S(1)}, bf16[64,4,1440]{2,1,0:T(4,128)(2,1)S(1)}, u32[]{:S(2)}, u32[]{:S(2)}) %collective-permute-start) | collective-permute-done | bytes 737312 | tf_op jit(solution)/shard_map/ppermute | solution.py:103
  76.1 19.0 %collective-permute-done.1 = bf16[64,4,1440]{2,1,0:T(4,128)(2,1)S(1)} collective-permute-done((bf16[64,4,1440]{2,1,0:T(4,128)(2,1)S(1)}, bf16[64,4,1440]{2,1,0:T(4,128)(2,1)S(1)}, u32[]{:S(2)}, u32[]{:S(2)}) %collective-permute-start.1) | collective-permute-done | bytes 737312 | tf_op jit(solution)/shard_map/ppermute | solution.py:103
  96.0 4.7 collective-permute-start.3
  102.2 12.3 %collective-permute-done.2 = bf16[64,4,1440]{2,1,0:T(4,128)(2,1)} collective-permute-done((bf16[64,4,1440]{2,1,0:T(4,128)(2,1)S(1)}, bf16[64,4,1440]{2,1,0:T(4,128)(2,1)}, u32[]{:S(2)}, u32[]{:S(2)}) %collective-permute-start.2) | collective-permute-done | bytes 737312 | tf_op jit(solution)/shard_map/ppermute | solution.py:103
  129.5 4.2 reshape.314
  133.7 4.1 multiply_convert_fusion
  141.1 7.2 %collective-permute-done.4 = bf16[1,360,1440]{2,1,0:T(8,128)(2,1)} collective-permute-done((bf16[1,360,1440]{2,1,0:T(8,128)(2,1)}, bf16[1,360,1440]{2,1,0:T(8,128)(2,1)}, u32[]{:S(2)}, u32[]{:S(2)}) %collective-permute-start.4) | collective-permute-done | bytes 1036832 | tf_op jit(solution)/shard_map/ppermute | solution.py:10
  154.5 8.0 %copy.63 = f32[256,4,1440]{2,1,0:T(4,128)} copy(f32[256,4,1440]{0,2,1:T(8,128)} %pad_maximum_fusion) | data formatting | bytes 11796480 | tf_op jit(solution)/shard_map/concatenate | solution.py:55
  162.4 4.9 slice.58
  167.3 4.6 copy.75
  171.9 4.1 reshape.318
  176.0 3.5 fusion.2
  188.4 7.9 %copy.70 = f32[256,4,1440]{2,1,0:T(4,128)} copy(f32[256,4,1440]{0,2,1:T(8,128)} %pad_maximum_fusion.1) | data formatting | bytes 11796480 | tf_op jit(solution)/shard_map/concatenate | solution.py:55
  196.3 213.9 %all-reduce.6 = (bf16[256,4,1440]{2,1,0:T(4,128)(2,1)}, bf16[256,4,1440]{2,1,0:T(4,128)(2,1)}) all-reduce(f32[256,4,1440]{2,1,0:T(4,128)} %copy.63, f32[256,4,1440]{2,1,0:T(4,128)} %copy.70), channel_id=2, replica_groups=mesh['expert'=64,'dp'=4] {'dp'}, use_global_device_ids=true, to_apply=%region_6.7.clone | all-reduce | flops 2949120 | bytes 17694720
  412.6 8.9 %all-to-all-start.3 = ((bf16[64,4,1440]{2,1,0:T(4,128)(2,1)}), bf16[64,4,1440]{2,1,0:T(4,128)(2,1)S(1)}, u32[]{:S(2)}, u32[]{:S(2)}) async-start(bf16[64,4,1440]{2,1,0:T(4,128)(2,1)} %dynamic-slice_convert_fusion), calls=%async_computation.3 | async-start | bytes 1572864 | tf_op jit(solution)/shard_map/all_to_all | solution.py:182
  428.3 16.1 %all-to-all-done.3 = bf16[64,4,1440]{2,1,0:T(4,128)(2,1)S(1)} async-done(((bf16[64,4,1440]{2,1,0:T(4,128)(2,1)}), bf16[64,4,1440]{2,1,0:T(4,128)(2,1)S(1)}, u32[]{:S(2)}, u32[]{:S(2)}) %all-to-all-start.3) | async-done | bytes 737312 | tf_op jit(solution)/shard_map/all_to_all | solution.py:182
  444.4 6.4 %all-to-all-start.1 = ((bf16[64,4,1440]{2,1,0:T(4,128)(2,1)}), bf16[64,4,1440]{2,1,0:T(4,128)(2,1)}, u32[]{:S(2)}, u32[]{:S(2)}) async-start(bf16[64,4,1440]{2,1,0:T(4,128)(2,1)} %dynamic-slice_convert_fusion.1), calls=%async_computation.1 | async-start | bytes 1572864 | tf_op jit(solution)/shard_map/all_to_all | solution.py:130
  454.5 3.8 collective-permute-done.6
  458.3 4.0 fusion.4
  462.3 27.4 %collective-permute-done.5 = bf16[1440,360]{1,0:T(8,128)(2,1)S(1)} collective-permute-done((bf16[1440,360]{1,0:T(8,128)(2,1)S(1)}, bf16[1440,360]{1,0:T(8,128)(2,1)S(1)}, u32[]{:S(2)}, u32[]{:S(2)}) %collective-permute-start.5) | collective-permute-done | bytes 1036832 | tf_op jit(solution)/shard_map/ppermute | solution.py:10
  (133 shorter events, 83.7 us)
Async XLA Ops:
  7.2 5.0 copy-start.16
  7.2 7.0 %copy-start.18 = (s32[8]{0:T(128)S(1)}, s32[8]{0:T(128)}, u32[]{:S(2)}) copy-start(s32[8]{0:T(128)} %param.14) | copy-start | bytes 100
  7.2 9.7 %copy-start.13 = (bf16[128,1440]{0,1:T(8,128)(2,1)S(1)}, bf16[128,1440]{0,1:T(8,128)(2,1)}, u32[]{:S(2)}) copy-start(bf16[128,1440]{0,1:T(8,128)(2,1)} %param.10) | copy-start | bytes 1105924
  18.7 14.5 %copy-start.14 = (bf16[128,1440]{0,1:T(8,128)(2,1)S(1)}, bf16[128,1440]{0,1:T(8,128)(2,1)}, u32[]{:S(2)}) copy-start(bf16[128,1440]{0,1:T(8,128)(2,1)} %param.17) | copy-start | bytes 1105924
  20.0 36.1 %all-to-all-start = ((bf16[64,4,1440]{2,1,0:T(4,128)(2,1)}), bf16[64,4,1440]{2,1,0:T(4,128)(2,1)S(1)}, u32[]{:S(2)}, u32[]{:S(2)}) async-start(bf16[64,4,1440]{2,1,0:T(4,128)(2,1)} %broadcast_select_fusion), calls=%async_computation | async-start | bytes 1572864 | tf_op jit(solution)/shard_map/all_to_all | solution.py:98
  34.6 22.7 %copy-start.17 = (s32[128,4]{0,1:T(4,128)S(1)}, s32[128,4]{0,1:T(4,128)}, u32[]{:S(2)}) copy-start(s32[128,4]{0,1:T(4,128)} %param.12) | copy-start | bytes 6148
  56.2 19.9 %collective-permute-start = (bf16[64,4,1440]{2,1,0:T(4,128)(2,1)S(1)}, bf16[64,4,1440]{2,1,0:T(4,128)(2,1)S(1)}, u32[]{:S(2)}, u32[]{:S(2)}) collective-permute-start(bf16[64,4,1440]{2,1,0:T(4,128)(2,1)S(1)} %all-to-all-done), channel_id=1, source_target_pairs={{0,1},{1,2},{2,3},{3,0},{4,5},{5,6},{6,7},{7,4},{8,9},{9,10},{10,1... | collective-permute-start | bytes 2211848 | tf_op jit(solution)/shard_map/ppermute | solution.py:103
  61.0 40.0 %copy-start.19 = (u32[256]{0:T(256)S(1)}, u32[256]{0:T(256)}, u32[]{:S(2)}) copy-start(u32[256]{0:T(256)} %constant.195) | copy-start | bytes 3076
  61.0 34.1 %all-to-all-start.2 = ((bf16[64,4,1440]{2,1,0:T(4,128)(2,1)}), bf16[64,4,1440]{2,1,0:T(4,128)(2,1)S(1)}, u32[]{:S(2)}, u32[]{:S(2)}) async-start(bf16[64,4,1440]{2,1,0:T(4,128)(2,1)} %select_convert_fusion), calls=%async_computation.2 | async-start | bytes 1572864 | tf_op jit(solution)/shard_map/all_to_all | solution.py:131
  67.6 94.8 %all-gather.2.cloned.1.call-start = ((), (), s32[]{:S(2)}) async-start(), calls=%async_computation.4 | async-start | bytes 3932160 | tf_op jit(solution)/shard_map/all_gather | solution.py:132
  76.1 19.0 %collective-permute-start.1 = (bf16[64,4,1440]{2,1,0:T(4,128)(2,1)S(1)}, bf16[64,4,1440]{2,1,0:T(4,128)(2,1)S(1)}, u32[]{:S(2)}, u32[]{:S(2)}) collective-permute-start(bf16[64,4,1440]{2,1,0:T(4,128)(2,1)S(1)} %collective-permute-done), channel_id=1, source_target_pairs={{0,1},{1,2},{2,3},{3,0},{4,5},{5,6},{6,7},{7,4},{8,9},{9,10},{10,1... | collective-permute-start | bytes 2211848 | tf_op jit(solution)/shard_map/ppermute | solution.py:103
  95.1 19.4 %collective-permute-start.2 = (bf16[64,4,1440]{2,1,0:T(4,128)(2,1)S(1)}, bf16[64,4,1440]{2,1,0:T(4,128)(2,1)}, u32[]{:S(2)}, u32[]{:S(2)}) collective-permute-start(bf16[64,4,1440]{2,1,0:T(4,128)(2,1)S(1)} %collective-permute-done.1), channel_id=1, source_target_pairs={{0,1},{1,2},{2,3},{3,0},{4,5},{5,6},{6,7},{7,4},{8,9},{9,10},{10,1... | collective-permute-start | bytes 2211848 | tf_op jit(solution)/shard_map/ppermute | solution.py:103
  96.0 43.2 %collective-permute-start.3 = (bf16[1,1440,360]{2,1,0:T(8,128)(2,1)}, bf16[1,1440,360]{2,1,0:T(8,128)(2,1)}, u32[]{:S(2)}, u32[]{:S(2)}) collective-permute-start(bf16[1,1440,360]{2,1,0:T(8,128)(2,1)} %param.15), channel_id=1, source_target_pairs={{0,128},{4,132},{8,136},{12,140},{16,144},{20,148},{24,152},{28,15... | collective-permute-start | bytes 3110408 | tf_op jit(solution)/shard_map/ppermute | solution.py:10
  100.7 47.6 %collective-permute-start.4 = (bf16[1,360,1440]{2,1,0:T(8,128)(2,1)}, bf16[1,360,1440]{2,1,0:T(8,128)(2,1)}, u32[]{:S(2)}, u32[]{:S(2)}) collective-permute-start(bf16[1,360,1440]{2,1,0:T(8,128)(2,1)} %param.16), channel_id=1, source_target_pairs={{0,128},{4,132},{8,136},{12,140},{16,144},{20,148},{24,152},{28,15... | collective-permute-start | bytes 3110408 | tf_op jit(solution)/shard_map/ppermute | solution.py:10
  141.1 9.1 %copy-start.6 = (bf16[1,360,1440]{2,1,0:T(8,128)(2,1)S(1)}, bf16[1,360,1440]{2,1,0:T(8,128)(2,1)}, u32[]{:S(2)}) copy-start(bf16[1,360,1440]{2,1,0:T(8,128)(2,1)} %param.16) | copy-start | bytes 3110404
  162.4 9.5 %copy-start = (bf16[256,4,1440]{2,1,0:T(4,128)(2,1)S(1)}, bf16[256,4,1440]{2,1,0:T(4,128)(2,1)}, u32[]{:S(2)}) copy-start(bf16[256,4,1440]{2,1,0:T(4,128)(2,1)} %all-gather.2.cloned.1.call-done) | copy-start | bytes 8847364
  410.2 11.2 %copy-start.9 = (bf16[256,1,1440]{0,2,1:T(8,128)(2,1)S(1)}, bf16[256,1,1440]{0,2,1:T(8,128)(2,1)}, u32[]{:S(2)}) copy-start(bf16[256,1,1440]{0,2,1:T(8,128)(2,1)} %copy.75) | copy-start | bytes 2211844
  412.6 31.9 %all-to-all-start.3 = ((bf16[64,4,1440]{2,1,0:T(4,128)(2,1)}), bf16[64,4,1440]{2,1,0:T(4,128)(2,1)S(1)}, u32[]{:S(2)}, u32[]{:S(2)}) async-start(bf16[64,4,1440]{2,1,0:T(4,128)(2,1)} %dynamic-slice_convert_fusion), calls=%async_computation.3 | async-start | bytes 1572864 | tf_op jit(solution)/shard_map/all_to_all | solution.py:182
  422.9 35.4 %collective-permute-start.6 = (bf16[360,1440]{1,0:T(8,128)(2,1)}, bf16[360,1440]{1,0:T(8,128)(2,1)}, u32[]{:S(2)}, u32[]{:S(2)}) collective-permute-start(bf16[360,1440]{1,0:T(8,128)(2,1)} %convolution_convert_fusion.1), channel_id=1, source_target_pairs={{0,128},{4,132},{8,136},{12,140},{16,144},{20,148},{24,152},{28,15... | collective-permute-start | bytes 3110408 | tf_op jit(solution)/shard_map/ppermute | solution.py:10
  425.9 24.9 %copy-start.2 = (bf16[256,1,1440]{0,2,1:T(8,128)(2,1)S(1)}, bf16[256,1,1440]{0,2,1:T(8,128)(2,1)}, u32[]{:S(2)}) copy-start(bf16[256,1,1440]{0,2,1:T(8,128)(2,1)} %copy.62) | copy-start | bytes 2211844
  428.3 30.0 %copy-start.12 = (bf16[768,360]{0,1:T(8,128)(2,1)S(1)}, bf16[768,360]{0,1:T(8,128)(2,1)}, u32[]{:S(2)}) copy-start(bf16[768,360]{0,1:T(8,128)(2,1)} %copy-done.11) | copy-start | bytes 1658884
  444.4 54.1 %all-to-all-start.1 = ((bf16[64,4,1440]{2,1,0:T(4,128)(2,1)}), bf16[64,4,1440]{2,1,0:T(4,128)(2,1)}, u32[]{:S(2)}, u32[]{:S(2)}) async-start(bf16[64,4,1440]{2,1,0:T(4,128)(2,1)} %dynamic-slice_convert_fusion.1), calls=%async_computation.1 | async-start | bytes 1572864 | tf_op jit(solution)/shard_map/all_to_all | solution.py:130
  451.4 38.3 %collective-permute-start.5 = (bf16[1440,360]{1,0:T(8,128)(2,1)S(1)}, bf16[1440,360]{1,0:T(8,128)(2,1)S(1)}, u32[]{:S(2)}, u32[]{:S(2)}) collective-permute-start(bf16[1440,360]{1,0:T(8,128)(2,1)S(1)} %convolution_convert_fusion), channel_id=1, source_target_pairs={{0,128},{4,132},{8,136},{12,140},{16,144},{20,148},{24,152},{28,15... | collective-permute-start | bytes 3110408 | tf_op jit(solution)/shard_map/ppermute | solution.py:10
  454.5 35.2 %copy-start.5 = (bf16[768,1440]{1,0:T(8,128)(2,1)S(1)}, bf16[768,1440]{1,0:T(8,128)(2,1)}, u32[]{:S(2)}) copy-start(bf16[768,1440]{1,0:T(8,128)(2,1)} %reshape.314) | copy-start | bytes 6635524
  (8 other events, 16.8 us)
Sparse Core Ops, SparseCore 0:
  96.1 45.3 all-gather.1
